TPU v7x, 128 devices: a whole 4x4x4 slice. The times are simulated.
128 devices in a mesh: seq: 8 (over x, core), exp: 16 (over y, z).
Axes of the slice: x: 4, y: 4, z: 4, core: 2. Of those that a mesh axis runs over, the one named last changes fastest.
Arguments:
- xin: bfloat16 [512, 4, 8192], P('seq', None, 'exp'), may hold values from -6 to 6
- zin: bfloat16 [512, 4, 8192], P('seq', None, 'exp'), may hold values from -6 to 6
- conv_weight: float32 [4, 8192], P(None, 'exp'), may hold values from -3 to 3
- conv_bias: float32 [8192], P('exp'), may hold values from -3 to 3
- xproj_weight: bfloat16 [8192, 288], P('exp'), may hold values from -0.0625 to 0.0625
- dtproj_weight: bfloat16 [256, 8192], P(None, 'exp'), may hold values from -0.375 to 0.375
- dt_bias: float32 [8192], P('exp'), may hold values from -5 to -3
- a_log: float32 [16, 8192], P(None, 'exp'), may hold values from -3 to 1
- skip: float32 [8192], P('exp'), may hold values from 0.2 to 1
- out_weight: bfloat16 [8192, 4096], P('exp'), may hold values from -0.0625 to 0.0625
- resid: bfloat16 [512, 4, 4096], P(('seq', 'exp')), may hold values from -6 to 6
- norm_gain: float32 [4096], replicated, may hold values from 0.5 to 1.5
- expert_ids: int32 [512, 4, 2], P(('seq', 'exp')), may hold values from 0 to 7, all different within a row; in each aligned block of 16 rows (0 to 15, 16 to 31, ..., all dimensions but the last counted through in order) at most 8 rows name the same one
- gate_weights: bfloat16 [512, 4, 2], P(('seq', 'exp')), may hold values from 0.19921875 to 1
- w_gate: bfloat16 [16, 4096, 6144], P('exp', None, 'seq'), may hold values from -0.09375 to 0.09375
- w_up: bfloat16 [16, 4096, 6144], P('exp', None, 'seq'), may hold values from -0.09375 to 0.09375
- w_down: bfloat16 [16, 6144, 4096], P('exp', 'seq'), may hold values from -0.0546875 to 0.0546875
Outputs:
- layer_out: bfloat16 [512, 4, 4096], P(('seq', 'exp'))
Inputs may be any that keep to these rules, and one draw needn't show every extreme that they name: `expert_ids`: tokens are ordered by position, then document; in each aligned block of 16 such tokens (the tokens of one device), every expert is named at most 8 times, and in every draw some expert is named exactly 8 times in some block. Each token names 2 different experts.
All inputs are finite; a program needn't handle non-finite values.
Results may differ from a plain program's by a relative error of at most 0.03.
Values may be sent and summed in bfloat16 or wider, within the bound.
No kernel may reach another device: no remote copies, remote signals or barrier semaphores. Data moves between devices by JAX's collectives and lax.ppermute only.
A program may use at most 128 MiB of HBM per device.

v0:
```python
import jax
import jax.numpy as jnp
from jax import lax
from jax.sharding import PartitionSpec as P

D = 4096
STATE = 16
CONV = 4
RANK = 256
EXPERTS = 8
TOPK = 2


def passed_along(value, axis, by):
    count = lax.axis_size(axis)
    pairs = [(i, i + by) for i in range(count) if 0 <= i + by < count]
    return lax.ppermute(value, axis, pairs)


def entering(value, axis, join, neutral):
    place = lax.axis_index(axis)
    gathered = jax.tree.map(
        lambda a, kind: lax.all_gather(a.astype(kind), axis), value, (jnp.bfloat16, jnp.bfloat16)
    )
    state = jax.tree.map(lambda a, e: jnp.zeros_like(a) + jnp.asarray(e, a.dtype), value, neutral)

    def one(step, state):
        return join(
            state,
            jax.tree.map(
                lambda a, own: lax.dynamic_index_in_dim(a, step, 0, False).astype(own.dtype),
                gathered,
                value,
            ),
        )

    return lax.fori_loop(0, place, one, state)


def conv_inputs(window, conv_weight, conv_bias, length):
    running = jnp.zeros(window[:length].shape, jnp.float32) + conv_bias
    for offset in range(CONV):
        running = running + conv_weight[offset] * window[offset : offset + length]
    return running


def make_step(decay_rate):

    def advance(carry_state, series_now):
        step_now, input_now, read_now, value_now = series_now
        factor = jnp.exp(step_now[:, None, :] * decay_rate[None])
        carry_state = (
            factor * carry_state + (step_now * value_now)[:, None, :] * input_now[:, :, None]
        )
        return (carry_state, jnp.sum(read_now[:, :, None] * carry_state, axis=1))

    return advance


def chain(earlier, later):
    return (earlier[0] * later[0], later[0] * earlier[1] + later[1])


def slot_select(route_ids, capacity):
    flat_ids = route_ids.reshape(-1)
    onehot = (flat_ids[:, None] == jnp.arange(EXPERTS, dtype=jnp.int32)[None, :]).astype(jnp.int32)
    before = jnp.sum((jnp.cumsum(onehot, axis=0) - onehot) * onehot, axis=1)
    target = flat_ids * capacity + before
    matches = jnp.arange(EXPERTS * capacity, dtype=jnp.int32)[:, None] == target[None, :]
    return matches.reshape(EXPERTS * capacity, route_ids.shape[0], route_ids.shape[1])


def per_device(
    xin,
    zin,
    conv_weight,
    conv_bias,
    xproj_weight,
    dtproj_weight,
    dt_bias,
    a_log,
    skip,
    out_weight,
    resid,
    norm_gain,
    expert_ids,
    gate_weights,
    w_gate,
    w_up,
    w_down,
):
    section = xin.shape[0]
    edge_rows = passed_along(xin[section - (CONV - 1) :], "seq", 1)
    window = jnp.concatenate([edge_rows, xin], axis=0).astype(jnp.float32)
    inner_act = jax.nn.silu(conv_inputs(window, conv_weight, conv_bias, section)).astype(
        jnp.bfloat16
    )
    inner_f = inner_act.astype(jnp.float32)
    projected = jnp.einsum(
        "pbc,cr->pbr", inner_act, xproj_weight, preferred_element_type=jnp.float32
    )
    projected = lax.psum(projected.astype(jnp.bfloat16), "exp").astype(jnp.float32)
    low_rank = projected[..., :RANK].astype(jnp.bfloat16)
    in_state = projected[..., RANK : RANK + STATE]
    out_state = projected[..., RANK + STATE :]
    step_size = jax.nn.softplus(
        jnp.einsum("pbr,rc->pbc", low_rank, dtproj_weight, preferred_element_type=jnp.float32)
        + dt_bias
    )
    decay_rate = -jnp.exp(a_log)
    advance = make_step(decay_rate)
    series = (step_size, in_state, out_state, inner_f)
    zero_state = jnp.zeros((xin.shape[1], STATE, xin.shape[2]), jnp.float32)
    final_local, local_out = lax.scan(advance, zero_state, series)
    total_decay = jnp.exp(jnp.sum(step_size, axis=0)[:, None, :] * decay_rate[None])
    identity = (jnp.ones_like(total_decay), jnp.zeros_like(final_local))
    incoming = entering((total_decay, final_local), "seq", chain, identity)[1]
    ignored, ssm_out = lax.scan(advance, incoming, series)
    mixed_in = ((ssm_out + skip * inner_f) * jax.nn.silu(zin.astype(jnp.float32))).astype(
        jnp.bfloat16
    )
    row_block = mixed_in
    mamba_rows = lax.psum_scatter(
        jnp.einsum("pbc,cd->pbd", row_block, out_weight, preferred_element_type=jnp.float32).astype(
            jnp.bfloat16
        ),
        "exp",
        scatter_dimension=0,
        tiled=True,
    ).astype(jnp.float32)
    hidden_state = resid.astype(jnp.float32) + mamba_rows
    norm_scale = lax.rsqrt(jnp.mean(hidden_state * hidden_state, axis=-1, keepdims=True) + 1e-05)
    normed = (hidden_state * norm_scale * norm_gain).astype(jnp.bfloat16)
    row_count = resid.shape[0] * resid.shape[1]
    capacity = 2 * TOPK * row_count // EXPERTS
    splits = lax.axis_size("exp") // EXPERTS
    tokens = normed.reshape(row_count, D)
    route_ids = expert_ids.reshape(row_count, TOPK)
    gate_vals = gate_weights.reshape(row_count, TOPK)
    matches = slot_select(route_ids, capacity)
    chosen = jnp.sum(matches.astype(jnp.int32), axis=2).astype(jnp.bfloat16)
    outgoing = (
        jnp.dot(chosen, tokens, preferred_element_type=jnp.float32)
        .astype(jnp.bfloat16)
        .reshape(EXPERTS, capacity, D)
    )
    arrived = lax.all_to_all(
        jnp.tile(outgoing, (splits, 1, 1)), "exp", split_axis=0, concat_axis=0, tiled=True
    )
    everything = lax.all_gather(arrived, "seq", axis=0, tiled=True)
    row_block = everything
    expert_row_block = row_block.reshape(-1, D)
    gate_act = jnp.dot(expert_row_block, w_gate[0], preferred_element_type=jnp.float32)
    up_act = jnp.dot(expert_row_block, w_up[0], preferred_element_type=jnp.float32)
    hidden = (jax.nn.silu(gate_act) * up_act).astype(jnp.bfloat16)
    own_rows = lax.psum_scatter(
        jnp.dot(hidden, w_down[0], preferred_element_type=jnp.float32)
        .reshape(lax.axis_size("seq") * arrived.shape[0], capacity, D)
        .astype(jnp.bfloat16),
        "seq",
        scatter_dimension=0,
        tiled=True,
    ).astype(jnp.float32)
    returned = lax.all_to_all(
        own_rows.astype(jnp.bfloat16), "exp", split_axis=0, concat_axis=0, tiled=True
    ).astype(own_rows.dtype)
    summed = jnp.sum(returned.reshape(splits, EXPERTS * capacity, D), axis=0)
    weights = jnp.sum(matches.astype(jnp.float32) * gate_vals.astype(jnp.float32)[None], axis=2)
    expert_out = jnp.dot(weights.T, summed, precision=lax.Precision.HIGHEST)
    return (hidden_state + expert_out.reshape(hidden_state.shape)).astype(jnp.bfloat16)


def solution(mesh):
    placed = (
        P("seq", None, "exp"),
        P("seq", None, "exp"),
        P(None, "exp"),
        P("exp"),
        P("exp", None),
        P(None, "exp"),
        P("exp"),
        P(None, "exp"),
        P("exp"),
        P("exp", None),
        P(("seq", "exp"), None, None),
        P(),
        P(("seq", "exp"), None, None),
        P(("seq", "exp"), None, None),
        P("exp", None, "seq"),
        P("exp", None, "seq"),
        P("exp", "seq", None),
    )
    return jax.shard_map(
        per_device,
        mesh=mesh,
        in_specs=placed,
        out_specs=P(("seq", "exp"), None, None),
        check_vma=False,
    )
```

profile of v0, /device:TPU:2, one launch (start us, length us, event | category | flops | bytes accessed | tf_op | source)
XLA Modules:
  0.0 485.4 jit_solution(7767882943626385610)
XLA Ops:
  6.6 0.8 slice.38
  7.4 1.9 collective-permute-start
  9.3 0.9 fusion.43
  10.2 2.2 collective-permute-done
  12.4 1.1 maximum_convert_fusion
  13.5 1.2 fusion.39
  14.7 1.0 convolution_convert_fusion.3
  15.8 86.0 %all-reduce.4.cloned.1.call-done = bf16[64,4,288]{2,0,1:T(8,128)(2,1)} async-done(((bf16[64,4,288]{2,0,1:T(8,128)(2,1)}), bf16[64,4,288]{2,0,1:T(8,128)(2,1)}) %all-reduce.4.cloned.1.call-update) | async-done | bytes 147472 | tf_op jit(solution)/shard_map/psum | solution.py:102
  101.8 1.2 fusion.35
  103.6 1.7 fusion.42
  105.4 10.3 %while.37 = (s32[]{:T(128)}, f32[4,16,512]{2,1,0:T(8,128)S(1)}, f32[64,4,512]{2,1,0:T(4,128)S(1)}, f32[16,512]{1,0:T(8,128)S(1)}, f32[64,4,512]{2,1,0:T(4,128)S(...) while((s32[]{:T(128)}, f32[4,16,512]{2,1,0:T(8,128)S(1)}, f32[64,4,512]{2,1,0:T(4,128)S(1)}, ...), condition=%wide.region_3.4_spmd.clone, body=%wide.region_2.3_spmd.clone.sunk | while | flops 165891 | bytes 353131 | solution.py:114
  115.7 13.1 %all-gather = bf16[32,16,512]{2,1,0:T(8,128)(2,1)S(1)} all-gather(bf16[4,16,512]{2,1,0:T(8,128)(2,1)S(1)} %convert_element_type.103), channel_id=2, replica_groups=mesh['seq'=8,'exp'=16] {'seq'}, dimensions={0}, use_global_device_ids=true | all-gather | bytes 589824 | tf_op jit(solution)/shard_map/all_gather | solution.py:23
  128.9 13.1 %all_gather.13 = bf16[8,4,16,512]{3,2,1,0:T(8,128)(2,1)S(1)} all-gather(bf16[1,4,16,512]{3,2,1,0:T(8,128)(2,1)S(1)} %exponential_convert_fusion), channel_id=1, replica_groups=mesh['seq'=8,'exp'=16] {'seq'}, dimensions={0}, use_global_device_ids=true | all-gather | bytes 589824 | tf_op jit(solution)/shard_map/all_gather | solution.py:23
  142.2 58.7 %while.36 = (s32[]{:T(128)}, f32[4,16,512]{2,1,0:T(8,128)S(1)}, f32[64,4,512]{2,1,0:T(4,128)S(1)}, f32[64,4,512]{2,1,0:T(4,128)S(1)}, f32[16,512]{1,0:T(8,128)S(...) while((s32[]{:T(128)}, f32[4,16,512]{2,1,0:T(8,128)S(1)}, ...), condition=%wide.region_8.9_spmd, body=%wide.region_6.8_spmd.sunk | while | flops 196610 | bytes 378481 | solution.py:118
  142.2 0.7 constant_dynamic-slice_fusion.3
  143.1 0.7 constant_dynamic-slice_fusion.3
  144.1 0.7 constant_dynamic-slice_fusion.3
  145.0 0.7 constant_dynamic-slice_fusion.3
  178.8 0.8 constant_dynamic-slice_fusion.3
  179.7 0.8 constant_dynamic-slice_fusion.3
  180.7 0.8 constant_dynamic-slice_fusion.3
  181.6 0.8 constant_dynamic-slice_fusion.3
  182.5 0.8 constant_dynamic-slice_fusion.3
  183.5 0.8 constant_dynamic-slice_fusion.3
  184.4 0.8 constant_dynamic-slice_fusion.3
  185.4 0.8 constant_dynamic-slice_fusion.3
  193.6 0.7 constant_dynamic-slice_fusion.3
  194.5 0.7 constant_dynamic-slice_fusion.3
  195.4 0.7 constant_dynamic-slice_fusion.3
  196.4 0.7 constant_dynamic-slice_fusion.3
  197.3 0.7 constant_dynamic-slice_fusion.3
  198.2 0.7 constant_dynamic-slice_fusion.3
  199.1 0.7 constant_dynamic-slice_fusion.3
  200.0 0.7 constant_dynamic-slice_fusion.3
  200.9 1.3 fusion.30
  202.3 4.8 convolution_convert_fusion.1
  209.3 87.8 %all-reduce.6.cloned.1.call-done = bf16[64,4,4096]{2,0,1:T(8,128)(2,1)} async-done(((bf16[64,4,4096]{2,0,1:T(8,128)(2,1)}), bf16[64,4,4096]{2,0,1:T(8,128)(2,1)}) %all-reduce.6.cloned.1.call-update) | async-done | bytes 2097168
  297.1 1.0 constant_dynamic-slice_fusion.1
  299.1 20.6 %all_to_all.10 = bf16[16,8,4096]{2,1,0:T(8,128)(2,1)} all-to-all(bf16[16,8,4096]{2,1,0:T(8,128)(2,1)S(1)} %bitcast.113), channel_id=1, replica_groups=mesh['seq'=8,'exp'=16] {'exp'}, dimensions={0} | all-to-all | bytes 2097152 | tf_op jit(solution)/shard_map/all_to_all | solution.py:147
  319.9 46.7 %all-gather.3.cloned.1.call-done = bf16[128,8,4096]{2,1,0:T(8,128)(2,1)} async-done(((bf16[16,8,4096]{2,1,0:T(8,128)(2,1)}), bf16[128,8,4096]{2,1,0:T(8,128)(2,1)}) %all-gather.3.cloned.1.call-update) | async-done | bytes 8388624 | tf_op jit(solution)/shard_map/all_gather | solution.py:150
  366.6 11.0 %fusion.1 = f32[1024,768]{1,0:T(8,128)S(1)} fusion(bf16[128,8,4096]{2,1,0:T(8,128)(2,1)} %all-gather.3.cloned.1.call-done, bf16[1,4096,768]{2,1,0:T(8,128)(2,1)} %param.38), kind=kOutput, calls=%fused_computation.14 | convolution fusion | flops 6442450944 | bytes 17825792 | tf_op jit(solution)/shard_map/dot_general | solution.py:154
  377.7 9.9 %fusion.16 = bf16[128,8,768]{2,1,0:T(8,128)(2,1)S(1)} fusion(f32[1024,768]{1,0:T(8,128)S(1)} %fusion.1, bf16[1,4096,768]{2,1,0:T(8,128)(2,1)} %param.37, bf16[128,8,4096]{2,1,0:T(8,128)(2,1)S(1)} %copy-done.9), kind=kOutput, calls=%fused_computation.31 | convolution fusion | flops 6447169536 | bytes 19398656 | tf_op jit(solution)/shard_map/dot_general | solution.py:153
  387.6 8.9 %convolution_convert_fusion = bf16[128,8,4096]{2,0,1:T(8,128)(2,1)} fusion(bf16[1,768,4096]{2,1,0:T(8,128)(2,1)S(1)} %bitcast.122, bf16[128,8,768]{2,1,0:T(8,128)(2,1)S(1)} %fusion.16), kind=kOutput, calls=%fused_computation.18 | convolution fusion | flops 6446645248 | bytes 16252928 | tf_op jit(solution)/shard_map/dot_general | solution.py:157
  396.5 51.1 %reduce-scatter.3.cloned.1.call-done = bf16[16,8,4096]{2,0,1:T(8,128)(2,1)} async-done(((bf16[128,8,4096]{2,0,1:T(8,128)(2,1)}), bf16[16,8,4096]{2,0,1:T(8,128)(2,1)}) %reduce-scatter.3.cloned.1.call-update) | async-done | bytes 1048592 | tf_op jit(solution)/shard_map/reduce_scatter | solution.py:156
  447.7 2.8 copy.87
  450.4 7.2 %all-to-all-start.1 = ((bf16[16,8,4096]{2,1,0:T(8,128)(2,1)}), bf16[16,8,4096]{2,1,0:T(8,128)(2,1)S(1)}, u32[]{:S(2)}, u32[]{:S(2)}) async-start(bf16[16,8,4096]{2,1,0:T(8,128)(2,1)} %copy.87), calls=%async_computation.2 | async-start | bytes 2097152 | tf_op jit(solution)/shard_map/all_to_all | solution.py:164
  457.9 19.5 %all-to-all-done.1 = bf16[16,8,4096]{2,1,0:T(8,128)(2,1)S(1)} async-done(((bf16[16,8,4096]{2,1,0:T(8,128)(2,1)}), bf16[16,8,4096]{2,1,0:T(8,128)(2,1)S(1)}, u32[]{:S(2)}, u32[]{:S(2)}) %all-to-all-start.1) | async-done | bytes 1048608 | tf_op jit(solution)/shard_map/all_to_all | solution.py:164
  477.5 1.4 fusion.9
  (690 shorter events, 53.2 us)
Async XLA Ops:
  6.5 8.1 %copy-start = (bf16[512,288]{0,1:T(8,128)(2,1)S(1)}, bf16[512,288]{0,1:T(8,128)(2,1)}, u32[]{:S(2)}) copy-start(bf16[512,288]{0,1:T(8,128)(2,1)} %param.27) | copy-start | bytes 884740
  6.5 9.2 %copy-start.3 = (f32[16,512]{1,0:T(8,128)S(1)}, f32[16,512]{1,0:T(8,128)}, u32[]{:S(2)}) copy-start(f32[16,512]{1,0:T(8,128)} %param.30) | copy-start | bytes 98308
  6.5 95.3 %copy-start.2 = (bf16[256,512]{1,0:T(8,128)(2,1)S(1)}, bf16[256,512]{1,0:T(8,128)(2,1)}, u32[]{:S(2)}) copy-start(bf16[256,512]{1,0:T(8,128)(2,1)} %param.28) | copy-start | bytes 786436
  6.5 95.3 %copy-start.6 = (f32[512]{0:T(512)S(1)}, f32[512]{0:T(512)}, u32[]{:S(2)}) copy-start(f32[512]{0:T(512)} %param.29) | copy-start | bytes 6148
  6.5 95.2 %all-reduce.4.cloned.1.call-start = ((), (), s32[]{:S(2)}) async-start(), calls=%async_computation.3 | async-start | bytes 393216 | tf_op jit(solution)/shard_map/psum | solution.py:102
  7.4 5.0 %collective-permute-start = (bf16[3,4,512]{2,1,0:T(4,128)(2,1)S(1)}, bf16[3,4,512]{2,1,0:T(4,128)(2,1)S(1)}, u32[]{:S(2)}, u32[]{:S(2)}) collective-permute-start(bf16[3,4,512]{2,1,0:T(4,128)(2,1)S(1)} %slice.38), channel_id=1, source_target_pairs={{0,16},{16,32},{32,48},{48,64},{64,80},{80,96},{96,112},{1,17},{17... | collective-permute-start | bytes 36872 | tf_op jit(solution)/shard_map/ppermute | solution.py:17
  15.7 281.4 %all-reduce.6.cloned.1.call-start = ((), (), s32[]{:S(2)}) async-start(), calls=%async_computation.6 | async-start | bytes 4194304
  105.3 95.6 %copy-start.7 = (f32[512]{0:T(512)S(1)}, f32[512]{0:T(512)}, u32[]{:S(2)}) copy-start(f32[512]{0:T(512)} %param.31) | copy-start | bytes 6148
  202.3 4.9 %copy-start.5 = (s32[4,4,2]{1,2,0:T(2,128)S(1)}, s32[4,4,2]{1,2,0:T(2,128)}, u32[]{:S(2)}) copy-start(s32[4,4,2]{1,2,0:T(2,128)} %param.35) | copy-start | bytes 388
  202.3 5.7 %copy-start.10 = (u32[128]{0:T(128)S(1)}, u32[128]{0:T(128)}, u32[]{:S(2)}) copy-start(u32[128]{0:T(128)} %constant.77) | copy-start | bytes 1540
  202.3 95.9 %copy-start.1 = (bf16[4,4,4096]{2,1,0:T(4,128)(2,1)S(1)}, bf16[4,4,4096]{2,1,0:T(4,128)(2,1)}, u32[]{:S(2)}) copy-start(bf16[4,4,4096]{2,1,0:T(4,128)(2,1)} %param.33) | copy-start | bytes 393220
  202.3 96.1 %copy-start.4 = (f32[4096]{0:T(1024)S(1)}, f32[4096]{0:T(1024)}, u32[]{:S(2)}) copy-start(f32[4096]{0:T(1024)} %param.34) | copy-start | bytes 49156
  207.1 159.5 %all-gather.3.cloned.1.call-start = ((), (), s32[]{:S(2)}) async-start(), calls=%async_computation.4 | async-start | bytes 9437184 | tf_op jit(solution)/shard_map/all_gather | solution.py:150
  319.7 128.0 %reduce-scatter.3.cloned.1.call-start = ((), (), s32[]{:S(2)}) async-start(), calls=%async_computation.5 | async-start | bytes 9437184 | tf_op jit(solution)/shard_map/reduce_scatter | solution.py:156
  366.6 11.0 %copy-start.9 = (bf16[128,8,4096]{2,1,0:T(8,128)(2,1)S(1)}, bf16[128,8,4096]{2,1,0:T(8,128)(2,1)}, u32[]{:S(2)}) copy-start(bf16[128,8,4096]{2,1,0:T(8,128)(2,1)} %all-gather.3.cloned.1.call-done) | copy-start | bytes 25165828
  366.6 21.0 %slice-start = ((s8[6291456]{0:T(1024)(128)(4,1)}), s8[4194304]{0:T(1024)(128)(4,1)S(1)}, s32[]{:S(2)}) async-start(s8[6291456]{0:T(1024)(128)(4,1)} %bitcast.121), calls=%async_computation.7 | async-start | bytes 8388608
  377.7 10.0 %slice-start.1 = ((s8[6291456]{0:T(1024)(128)(4,1)}), s8[2097152]{0:T(1024)(128)(4,1)S(1)}, s32[]{:S(2)}) async-start(s8[6291456]{0:T(1024)(128)(4,1)} %bitcast.121), calls=%async_computation.8 | async-start | bytes 4194304
  396.5 61.2 %copy-start.8 = (bf16[4,4,2]{1,2,0:T(2,128)(2,1)S(1)}, bf16[4,4,2]{1,2,0:T(2,128)(2,1)}, u32[]{:S(2)}) copy-start(bf16[4,4,2]{1,2,0:T(2,128)(2,1)} %param.36) | copy-start | bytes 196
  450.4 26.9 %all-to-all-start.1 = ((bf16[16,8,4096]{2,1,0:T(8,128)(2,1)}), bf16[16,8,4096]{2,1,0:T(8,128)(2,1)S(1)}, u32[]{:S(2)}, u32[]{:S(2)}) async-start(bf16[16,8,4096]{2,1,0:T(8,128)(2,1)} %copy.87), calls=%async_computation.2 | async-start | bytes 2097152 | tf_op jit(solution)/shard_map/all_to_all | solution.py:164
Sparse Core Ops, SparseCore 0:
  15.8 85.9 all-reduce.3
  207.3 89.8 all-reduce.5
  319.8 46.7 all-gather.2
  396.7 50.9 reduce-scatter.2
where the time goes:
time: 489 us; the launch traced here: 485 us
  waiting for transfers between devices  293 us (60%)
  local copies, waits for them, and re-layouts  58.7 us (12%)
  blocking collectives  46.9 us (10%)
  matrix products  38.5 us (8%)
  other arithmetic  19.2 us (4%)
  between operations  14.1 us (3%)
  starting transfers between devices  9.47 us (2%)
  loops' own time  5.32 us (1%)
    unnamed x5, waiting for transfers between devices  87.8 us
    psum x1, waiting for transfers between devices, per_device(): lax.psum(projected.astype(jnp.bfloat16), 'exp').astype(jnp.float32)  86 us
    reduce_scatter x1, waiting for transfers between devices, per_device(): lax.psum_scatter(jnp.dot(hidden, w_down[0], preferred_element_type=jnp.fl...  51.1 us
    dynamic_slice x64, local copies, waits for them, and re-layouts, per_device(): final_local, local_out = lax.scan(advance, zero_state, series)  47 us
    all_gather x1, waiting for transfers between devices, per_device(): everything = lax.all_gather(arrived, 'seq', axis=0, tiled=True)  46.7 us
    all_gather x2, blocking collectives, entering(): lax.all_gather(a.astype(kind), axis)  26.2 us
    all_to_all x1, blocking collectives, per_device(): lax.all_to_all(jnp.tile(outgoing, (splits, 1, 1)), 'exp', split_axis=0, c...  20.6 us
    all_to_all x1, waiting for transfers between devices, per_device(): lax.all_to_all(own_rows.astype(jnp.bfloat16), 'exp', split_axis=0, concat...  19.5 us
  transfers between devices with their start and end apart: 6, of which 6 were waited for; matrix products, arithmetic and copies ran while one was open for 1% of the time, Pallas kernels for 0%

commit v1 on v0

--- a/solution.py
+++ b/solution.py
@@ -147,7 +147,9 @@
     arrived = lax.all_to_all(
         jnp.tile(outgoing, (splits, 1, 1)), "exp", split_axis=0, concat_axis=0, tiled=True
     )
-    everything = lax.all_gather(arrived, "seq", axis=0, tiled=True)
+    everything = jnp.concatenate(
+        lax.all_to_all(jnp.stack([arrived] * lax.axis_size("seq")), "seq", 0, 0), axis=0
+    )
     row_block = everything
     expert_row_block = row_block.reshape(-1, D)
     gate_act = jnp.dot(expert_row_block, w_gate[0], preferred_element_type=jnp.float32)

time: 489 us -> 574 us (1.17)
  blocking collectives: 46.9 us -> 146 us
  waiting for transfers between devices: 293 us -> 243 us
  local copies, waits for them, and re-layouts: 58.7 us -> 101 us
    all_to_all x0 -> x1, blocking collectives: none -> 99.4 us  [per_device(): lax.all_to_all(jnp.stack([arrived] * lax.axis_size('seq')), 'seq', 0, 0)]
    mul x128, local copies, waits for them, and re-layouts: 0.74 us -> 88.1 us  [advance(): (step_now * value_now)[:, None, :] * input_now[:, :, None]]
    all_gather x1 -> x0, waiting for transfers between devices: 46.7 us -> none  [per_device(): everything = lax.all_gather(arrived, 'seq', axis=0, tiled=True)]
    dynamic_slice x64, local copies, waits for them, and re-layouts: 47 us -> 0.88 us  [per_device(): final_local, local_out = lax.scan(advance, zero_state, series)]
    unnamed x5 -> x4, waiting for transfers between devices: 87.8 us -> 87.8 us
  transfers between devices with their start and end apart: 6 -> 5, of which waited for: 6 -> 5; matrix products, arithmetic and copies ran while one was open for 1% -> 0% of each run, Pallas kernels for 0% -> 0%
where the time goes in v1:
time: 574 us; the launch traced here: 571 us
  waiting for transfers between devices  243 us (42%)
  blocking collectives  146 us (25%)
  local copies, waits for them, and re-layouts  101 us (18%)
  matrix products  34.6 us (6%)
  other arithmetic  18.2 us (3%)
  between operations  14.2 us (2%)
  starting transfers between devices  9.26 us (2%)
    all_to_all x1, blocking collectives, per_device(): lax.all_to_all(jnp.stack([arrived] * lax.axis_size('seq')), 'seq', 0, 0)  99.4 us
    mul x128, local copies, waits for them, and re-layouts, advance(): (step_now * value_now)[:, None, :] * input_now[:, :, None]  88.1 us
    unnamed x4, waiting for transfers between devices  87.8 us
    psum x1, waiting for transfers between devices, per_device(): lax.psum(projected.astype(jnp.bfloat16), 'exp').astype(jnp.float32)  86 us
    reduce_scatter x1, waiting for transfers between devices, per_device(): lax.psum_scatter(jnp.dot(hidden, w_down[0], preferred_element_type=jnp.fl...  47.1 us
    all_gather x2, blocking collectives, entering(): lax.all_gather(a.astype(kind), axis)  26.2 us
    all_to_all x1, blocking collectives, per_device(): lax.all_to_all(jnp.tile(outgoing, (splits, 1, 1)), 'exp', split_axis=0, c...  20.5 us
    all_to_all x1, waiting for transfers between devices, per_device(): lax.all_to_all(own_rows.astype(jnp.bfloat16), 'exp', split_axis=0, concat...  19.5 us
  transfers between devices with their start and end apart: 5, of which 5 were waited for; matrix products, arithmetic and copies ran while one was open for 0% of the time, Pallas kernels for 0%

profile of v1, /device:TPU:2, one launch (start us, length us, event | category | flops | bytes accessed | tf_op | source)
XLA Modules:
  0.0 570.8 jit_solution(6527493295630914067)
XLA Ops:
  6.6 0.8 slice.38
  7.4 1.9 collective-permute-start
  9.3 0.9 fusion.37
  10.2 2.2 collective-permute-done
  12.4 1.1 maximum_convert_fusion
  13.5 1.2 fusion.33
  14.7 1.0 convolution_convert_fusion.3
  15.7 86.0 %all-reduce.4.cloned.1.call-done = bf16[64,4,288]{2,0,1:T(8,128)(2,1)} async-done(((bf16[64,4,288]{2,0,1:T(8,128)(2,1)}), bf16[64,4,288]{2,0,1:T(8,128)(2,1)}) %all-reduce.4.cloned.1.call-update) | async-done | bytes 147472 | tf_op jit(solution)/shard_map/psum | solution.py:102
  101.8 1.2 fusion.29
  103.6 1.0 fusion.36
  104.7 0.7 copy.75
  105.4 52.9 %while.37 = (s32[]{:T(128)}, f32[4,16,512]{2,1,0:T(8,128)S(1)}, f32[64,4,512]{2,1,0:T(4,128)S(1)}, f32[16,512]{1,0:T(8,128)S(1)}, f32[64,4,512]{2,1,0:T(4,128)S(...) while((s32[]{:T(128)}, f32[4,16,512]{2,1,0:T(8,128)S(1)}, f32[64,4,512]{2,1,0:T(4,128)S(1)}, ...), condition=%wide.region_3.4_spmd.clone, body=%wide.region_2.3_spmd.clone.sunk | while | flops 165891 | bytes 353131 | solution.py:114
  106.2 0.7 dynamic-slice_bitcast_fusion.10
  107.1 0.7 dynamic-slice_bitcast_fusion.10
  107.9 0.7 dynamic-slice_bitcast_fusion.10
  108.7 0.7 dynamic-slice_bitcast_fusion.10
  109.5 0.7 dynamic-slice_bitcast_fusion.10
  110.4 0.7 dynamic-slice_bitcast_fusion.10
  111.2 0.7 dynamic-slice_bitcast_fusion.10
  112.0 0.7 dynamic-slice_bitcast_fusion.10
  112.9 0.7 dynamic-slice_bitcast_fusion.10
  113.7 0.7 dynamic-slice_bitcast_fusion.10
  114.5 0.7 dynamic-slice_bitcast_fusion.10
  115.3 0.7 dynamic-slice_bitcast_fusion.10
  116.2 0.7 dynamic-slice_bitcast_fusion.10
  122.8 0.7 dynamic-slice_bitcast_fusion.10
  138.5 0.7 dynamic-slice_bitcast_fusion.10
  154.2 0.7 dynamic-slice_bitcast_fusion.10
  158.3 13.1 %all-gather = bf16[32,16,512]{2,1,0:T(8,128)(2,1)S(1)} all-gather(bf16[4,16,512]{2,1,0:T(8,128)(2,1)S(1)} %convert_element_type.103), channel_id=2, replica_groups=mesh['seq'=8,'exp'=16] {'seq'}, dimensions={0}, use_global_device_ids=true | all-gather | bytes 589824 | tf_op jit(solution)/shard_map/all_gather | solution.py:23
  171.4 13.1 %all_gather.10 = bf16[8,4,16,512]{3,2,1,0:T(8,128)(2,1)S(1)} all-gather(bf16[1,4,16,512]{3,2,1,0:T(8,128)(2,1)S(1)} %exponential_convert_fusion), channel_id=1, replica_groups=mesh['seq'=8,'exp'=16] {'seq'}, dimensions={0}, use_global_device_ids=true | all-gather | bytes 589824 | tf_op jit(solution)/shard_map/all_gather | solution.py:23
  184.7 57.0 %while.36 = (s32[]{:T(128)}, f32[4,16,512]{2,1,0:T(8,128)S(1)}, f32[64,4,512]{2,1,0:T(4,128)S(1)}, f32[64,4,512]{2,1,0:T(4,128)S(1)}, f32[16,512]{1,0:T(8,128)S(...) while((s32[]{:T(128)}, f32[4,16,512]{2,1,0:T(8,128)S(1)}, ...), condition=%wide.region_8.9_spmd, body=%wide.region_6.8_spmd.sunk | while | flops 196610 | bytes 378481 | solution.py:118
  196.4 0.7 dynamic-slice_bitcast_fusion.8
  213.3 0.7 dynamic-slice_bitcast_fusion.8
  230.3 0.7 dynamic-slice_bitcast_fusion.8
  242.2 4.8 convolution_convert_fusion.1
  249.3 87.7 %all-reduce.6.cloned.1.call-done = bf16[64,4,4096]{2,0,1:T(8,128)(2,1)} async-done(((bf16[64,4,4096]{2,0,1:T(8,128)(2,1)}), bf16[64,4,4096]{2,0,1:T(8,128)(2,1)}) %all-reduce.6.cloned.1.call-update) | async-done | bytes 2097168
  337.0 1.0 constant_dynamic-slice_fusion.1
  338.9 20.5 %all_to_all.15 = bf16[16,8,4096]{2,1,0:T(8,128)(2,1)S(1)} all-to-all(bf16[16,8,4096]{2,1,0:T(8,128)(2,1)S(1)} %bitcast.109), channel_id=1, replica_groups=mesh['seq'=8,'exp'=16] {'exp'}, dimensions={0} | all-to-all | bytes 2097152 | tf_op jit(solution)/shard_map/all_to_all | solution.py:147
  359.5 1.0 stack.2
  360.5 99.4 %all_to_all.16 = bf16[8,16,8,4096]{3,2,1,0:T(8,128)(2,1)S(1)} all-to-all(bf16[8,16,8,4096]{3,2,1,0:T(8,128)(2,1)S(1)} %stack.2), channel_id=1, replica_groups=mesh['seq'=8,'exp'=16] {'seq'}, dimensions={0} | all-to-all | bytes 16777216 | tf_op jit(solution)/shard_map/all_to_all | solution.py:151
  459.9 8.3 %fusion.2 = f32[1024,768]{1,0:T(8,128)} fusion(bf16[1024,4096]{1,0:T(8,128)(2,1)S(1)} %bitcast.106, bf16[1,4096,768]{2,1,0:T(8,128)(2,1)S(1)} %bitcast.118), kind=kOutput, calls=%fused_computation.16 | convolution fusion | flops 6442450944 | bytes 17825792 | tf_op jit(solution)/shard_map/dot_general | solution.py:156
  468.2 8.8 %fusion.12 = bf16[128,8,768]{2,1,0:T(8,128)(2,1)S(1)} fusion(f32[1024,768]{1,0:T(8,128)} %fusion.2, bf16[1024,4096]{1,0:T(8,128)(2,1)S(1)} %bitcast.107, bf16[1,4096,768]{2,1,0:T(8,128)(2,1)S(1)} %bitcast.120), kind=kOutput, calls=%fused_computation.29 | convolution fusion | flops 6447169536 | bytes 19398656 | tf_op jit(solution)/shard_map/dot_general | solution.py:155
  477.0 8.9 %convolution_convert_fusion = bf16[128,8,4096]{2,0,1:T(8,128)(2,1)} fusion(bf16[1,768,4096]{2,1,0:T(8,128)(2,1)S(1)} %bitcast.122, bf16[128,8,768]{2,1,0:T(8,128)(2,1)S(1)} %fusion.12), kind=kOutput, calls=%fused_computation.14 | convolution fusion | flops 6446645248 | bytes 16252928 | tf_op jit(solution)/shard_map/dot_general | solution.py:159
  486.0 47.1 %reduce-scatter.3.cloned.1.call-done = bf16[16,8,4096]{2,0,1:T(8,128)(2,1)} async-done(((bf16[128,8,4096]{2,0,1:T(8,128)(2,1)}), bf16[16,8,4096]{2,0,1:T(8,128)(2,1)}) %reduce-scatter.3.cloned.1.call-update) | async-done | bytes 1048592 | tf_op jit(solution)/shard_map/reduce_scatter | solution.py:158
  533.0 2.8 copy.87
  535.8 7.2 %all-to-all-start.2 = ((bf16[16,8,4096]{2,1,0:T(8,128)(2,1)}), bf16[16,8,4096]{2,1,0:T(8,128)(2,1)S(1)}, u32[]{:S(2)}, u32[]{:S(2)}) async-start(bf16[16,8,4096]{2,1,0:T(8,128)(2,1)} %copy.87), calls=%async_computation.3 | async-start | bytes 2097152 | tf_op jit(solution)/shard_map/all_to_all | solution.py:166
  543.2 19.5 %all-to-all-done.2 = bf16[16,8,4096]{2,1,0:T(8,128)(2,1)S(1)} async-done(((bf16[16,8,4096]{2,1,0:T(8,128)(2,1)}), bf16[16,8,4096]{2,1,0:T(8,128)(2,1)S(1)}, u32[]{:S(2)}, u32[]{:S(2)}) %all-to-all-start.2) | async-done | bytes 1048608 | tf_op jit(solution)/shard_map/all_to_all | solution.py:166
  562.9 1.4 fusion.7
  (701 shorter events, 96.3 us)
Async XLA Ops:
  6.5 8.1 %copy-start = (bf16[512,288]{0,1:T(8,128)(2,1)S(1)}, bf16[512,288]{0,1:T(8,128)(2,1)}, u32[]{:S(2)}) copy-start(bf16[512,288]{0,1:T(8,128)(2,1)} %param.27) | copy-start | bytes 884740
  6.5 9.2 %copy-start.5 = (f32[16,512]{1,0:T(8,128)S(1)}, f32[16,512]{1,0:T(8,128)}, u32[]{:S(2)}) copy-start(f32[16,512]{1,0:T(8,128)} %param.30) | copy-start | bytes 98308
  6.5 95.2 %copy-start.4 = (bf16[256,512]{1,0:T(8,128)(2,1)S(1)}, bf16[256,512]{1,0:T(8,128)(2,1)}, u32[]{:S(2)}) copy-start(bf16[256,512]{1,0:T(8,128)(2,1)} %param.28) | copy-start | bytes 786436
  6.5 95.2 %copy-start.8 = (f32[512]{0:T(512)S(1)}, f32[512]{0:T(512)}, u32[]{:S(2)}) copy-start(f32[512]{0:T(512)} %param.29) | copy-start | bytes 6148
  6.5 95.2 %all-reduce.4.cloned.1.call-start = ((), (), s32[]{:S(2)}) async-start(), calls=%async_computation.4 | async-start | bytes 393216 | tf_op jit(solution)/shard_map/psum | solution.py:102
  7.4 5.0 collective-permute-start
  15.7 321.3 %all-reduce.6.cloned.1.call-start = ((), (), s32[]{:S(2)}) async-start(), calls=%async_computation.6 | async-start | bytes 4194304
  104.6 137.1 %copy-start.3 = (bf16[64,4,512]{2,1,0:T(4,128)(2,1)S(1)}, bf16[64,4,512]{2,1,0:T(4,128)(2,1)}, u32[]{:S(2)}) copy-start(bf16[64,4,512]{2,1,0:T(4,128)(2,1)} %param.24) | copy-start | bytes 786436
  104.7 137.1 %copy-start.9 = (f32[512]{0:T(512)S(1)}, f32[512]{0:T(512)}, u32[]{:S(2)}) copy-start(f32[512]{0:T(512)} %param.31) | copy-start | bytes 6148
  242.2 4.9 copy-start.7
  242.2 5.7 %copy-start.11 = (u32[128]{0:T(128)S(1)}, u32[128]{0:T(128)}, u32[]{:S(2)}) copy-start(u32[128]{0:T(128)} %constant.77) | copy-start | bytes 1540
  242.2 95.8 %copy-start.2 = (bf16[4,4,4096]{2,1,0:T(4,128)(2,1)S(1)}, bf16[4,4,4096]{2,1,0:T(4,128)(2,1)}, u32[]{:S(2)}) copy-start(bf16[4,4,4096]{2,1,0:T(4,128)(2,1)} %param.33) | copy-start | bytes 393220
  242.2 96.1 %copy-start.6 = (f32[4096]{0:T(1024)S(1)}, f32[4096]{0:T(1024)}, u32[]{:S(2)}) copy-start(f32[4096]{0:T(1024)} %param.34) | copy-start | bytes 49156
  247.1 286.0 %reduce-scatter.3.cloned.1.call-start = ((), (), s32[]{:S(2)}) async-start(), calls=%async_computation.5 | async-start | bytes 9437184 | tf_op jit(solution)/shard_map/reduce_scatter | solution.py:158
  359.5 100.4 %slice-start = ((s8[6291456]{0:T(1024)(128)(4,1)}), s8[2097152]{0:T(1024)(128)(4,1)S(1)}, s32[]{:S(2)}) async-start(s8[6291456]{0:T(1024)(128)(4,1)} %bitcast.117), calls=%async_computation.7 | async-start | bytes 4194304
  360.5 99.4 %slice-start.1 = ((s8[6291456]{0:T(1024)(128)(4,1)}), s8[4194304]{0:T(1024)(128)(4,1)S(1)}, s32[]{:S(2)}) async-start(s8[6291456]{0:T(1024)(128)(4,1)} %bitcast.117), calls=%async_computation.8 | async-start | bytes 8388608
  360.5 107.7 %slice-start.2 = ((s8[6291456]{0:T(1024)(128)(4,1)}), s8[4194304]{0:T(1024)(128)(4,1)S(1)}, s32[]{:S(2)}) async-start(s8[6291456]{0:T(1024)(128)(4,1)} %bitcast.119), calls=%async_computation.9 | async-start | bytes 8388608
  459.9 8.3 %slice-start.3 = ((s8[6291456]{0:T(1024)(128)(4,1)}), s8[2097152]{0:T(1024)(128)(4,1)S(1)}, s32[]{:S(2)}) async-start(s8[6291456]{0:T(1024)(128)(4,1)} %bitcast.119), calls=%async_computation.10 | async-start | bytes 4194304
  459.9 17.1 %slice-start.4 = ((s8[6291456]{0:T(1024)(128)(4,1)}), s8[4194304]{0:T(1024)(128)(4,1)S(1)}, s32[]{:S(2)}) async-start(s8[6291456]{0:T(1024)(128)(4,1)} %bitcast.121), calls=%async_computation.11 | async-start | bytes 8388608
  468.2 8.8 %slice-start.5 = ((s8[6291456]{0:T(1024)(128)(4,1)}), s8[2097152]{0:T(1024)(128)(4,1)S(1)}, s32[]{:S(2)}) async-start(s8[6291456]{0:T(1024)(128)(4,1)} %bitcast.121), calls=%async_computation.12 | async-start | bytes 4194304
  485.9 57.1 %copy-start.10 = (bf16[4,4,2]{1,2,0:T(2,128)(2,1)S(1)}, bf16[4,4,2]{1,2,0:T(2,128)(2,1)}, u32[]{:S(2)}) copy-start(bf16[4,4,2]{1,2,0:T(2,128)(2,1)} %param.36) | copy-start | bytes 196
  486.0 78.3 %copy-start.1 = (bf16[512,288]{0,1:T(8,128)(2,1)S(1)}, bf16[512,288]{0,1:T(8,128)(2,1)}, u32[]{:S(2)}) copy-start(bf16[512,288]{0,1:T(8,128)(2,1)} %param.27) | copy-start | bytes 884740
  535.8 26.9 %all-to-all-start.2 = ((bf16[16,8,4096]{2,1,0:T(8,128)(2,1)}), bf16[16,8,4096]{2,1,0:T(8,128)(2,1)S(1)}, u32[]{:S(2)}, u32[]{:S(2)}) async-start(bf16[16,8,4096]{2,1,0:T(8,128)(2,1)} %copy.87), calls=%async_computation.3 | async-start | bytes 2097152 | tf_op jit(solution)/shard_map/all_to_all | solution.py:166
Sparse Core Ops, SparseCore 0:
  15.8 85.9 all-reduce.3
  247.2 89.7 all-reduce.5
  486.1 46.9 reduce-scatter.2
